TPU v7x, 512 devices: a whole 4x8x8 slice. The times are simulated.
512 devices in a mesh: sec: 16 (over z_lo, y), xs: 32 (over z_hi, x, core).
Axes of the slice: x: 4, y: 8, z: 8 (z_hi: 4, z_lo: 2; z = z_hi * 2 + z_lo), core: 2. Of those that a mesh axis runs over, the one named last changes fastest.
Arguments:
- soot: float32 [96, 512, 1024], P('sec', 'xs'), may hold values from 0.05 to 1
- species: float32 [40, 512, 1024], P(None, 'xs'), may hold values from 0.1 to 1
- kernel: float32 [96, 96], replicated, may hold values from 0.002 to 0.02
- split: float32 [96, 96], replicated, may hold values from 0.2 to 0.8
- target: int32 [96, 96], replicated, may hold values from 0 to 94, as said below
- growth: float32 [96], replicated, may hold values from 0.05 to 0.5
- diffusivity: float32 [40], replicated, may hold values from 0.05 to 0.2
- reaction: float32 [40, 40], replicated, may hold values from -1 to 1
- stoich: float32 [40], replicated, may hold values from -1 to 1
Outputs:
- soot_out: float32 [96, 512, 1024], P('sec', 'xs')
- species_out: float32 [40, 512, 1024], P(None, 'xs')
Inputs may be any that keep to these rules, and one draw needn't show every extreme that they name: target[i, j] = min(max(i, j) + r, 94) with r of 0 to 3.
All inputs are finite; a program needn't handle non-finite values.
Results may differ from a plain program's by a relative error of at most 0.0003.
Values sent between devices are 32-bit elements; how exact they have to be, the bound alone decides.
A program may use at most 128 MiB of HBM per device.

v0:
```python
import jax
import jax.numpy as jnp
from jax import lax
from jax.sharding import PartitionSpec as P

HI = lax.Precision.HIGHEST


def extended(cells, sides, width):
    for axis, dim in sides:
        count = lax.axis_size(axis)
        ends = count - 1
        head = lax.slice_in_dim(cells, 0, width, axis=dim)
        tail = lax.slice_in_dim(cells, cells.shape[dim] - width, cells.shape[dim], axis=dim)
        cells = jnp.concatenate(
            [
                lax.ppermute(tail, axis, [(i, (i + 1) % count) for i in range(ends)]),
                cells,
                lax.ppermute(head, axis, [((i + 1) % count, i) for i in range(ends)]),
            ],
            axis=dim,
        )
    return cells


def birth_rows(dense, kernel, split, target, first, count):

    def one_target(index):
        weights = (
            0.5
            * kernel
            * (
                split * (target == index).astype(kernel.dtype)
                + (1.0 - split) * (target + 1 == index).astype(kernel.dtype)
            )
        )
        product = jnp.dot(weights, dense, precision=HI)
        return jnp.sum(dense * product, axis=0)

    indices = first + jnp.arange(count)
    return lax.map(one_target, indices)


def shards(soot, species, kernel, split, target, growth, diffusivity, reaction, stoich):
    local_sec, rows, width = soot.shape
    kinds = species.shape[0]
    sections = kernel.shape[0]
    cells = rows * width
    flat = soot.reshape(local_sec, cells)
    acet = species[0].reshape(1, cells)
    whole = lax.all_gather(flat, "sec", axis=0, tiled=True)
    start = lax.axis_index("sec") * local_sec
    birth = birth_rows(whole, kernel, split, target, start, local_sec)
    kernel_rows = lax.dynamic_slice(kernel, (start, jnp.int32(0)), (local_sec, sections))
    loss = flat * jnp.dot(kernel_rows, whole, precision=HI)
    grow_own = lax.dynamic_slice_in_dim(growth, start, local_sec)
    flux = grow_own[:, None] * flat * acet
    before = jnp.maximum(start - 1, 0)
    prev_dense = lax.dynamic_slice(whole, (before, jnp.int32(0)), (1, cells))
    prev_rate = lax.dynamic_slice_in_dim(growth, before, 1)
    present = (start > 0).astype(flat.dtype)
    prev_flux = present * prev_rate[:, None] * prev_dense * acet
    inflow = jnp.concatenate([prev_flux, flux[:-1]], axis=0)
    rate = birth - loss - flux + inflow
    consumption = lax.psum(jnp.sum(flux, axis=0), "sec")
    stacked = jnp.concatenate([soot, species], axis=0)
    padded = extended(stacked, (("xs", 1),), 1)
    middle = jnp.pad(padded[:, 1:-1, :], ((0, 0), (0, 0), (1, 1)))
    beside = padded[:, 2:, :] + padded[:, :-2, :] + middle[:, :, 2:] + middle[:, :, :-2]
    lapl = beside - 4.0 * stacked
    soot_out = soot + 0.1 * lapl[:local_sec] + rate.reshape(soot.shape)
    mixed = jnp.dot(reaction, species.reshape(kinds, cells), precision=HI).reshape(species.shape)
    species_out = (
        species
        + diffusivity[:, None, None] * lapl[local_sec:]
        + mixed
        - stoich[:, None, None] * consumption.reshape(1, rows, width)
    )
    return (soot_out, species_out)


def solution(mesh):
    return jax.shard_map(
        shards,
        mesh=mesh,
        in_specs=(P("sec", "xs", None), P(None, "xs", None), P(), P(), P(), P(), P(), P(), P()),
        out_specs=(P("sec", "xs", None), P(None, "xs", None)),
        check_vma=False,
    )
```

profile of v0, /device:TPU:1, one launch (start us, length us, event | category | flops | bytes accessed | tf_op | source)
XLA Modules:
  0.0 338.9 jit_solution(17445586120005324353)
XLA Ops:
  7.2 0.9 slice_bitcast_fusion
  8.1 0.7 dynamic_slice.17
  8.8 1.7 multiply_reduce_fusion
  10.6 2.0 reshape.38
  12.7 1.2 copy.28
  13.9 3.5 %copy.27 = f32[40,16,1024]{2,0,1:T(8,128)S(1)} copy(f32[40,16,1024]{2,1,0:T(8,128)} %param.12) | data formatting | bytes 5242880 | tf_op args[1]
  17.4 0.7 fusion.32
  18.1 4.5 %collective-permute-start.1 = (f32[46,1,1024]{2,0,1:T(8,128)}, f32[46,1,1024]{2,0,1:T(8,128)}, u32[]{:S(2)}, u32[]{:S(2)}) collective-permute-start(f32[46,1,1024]{2,0,1:T(8,128)} %get-tuple-element.61), channel_id=1, source_target_pairs={{0,1},{1,2},{2,3},{3,4},{4,5},{5,6},{6,7},{7,8},{8,9},{9,10},{10,1... | collective-permute-start | bytes 565256 | tf_op jit(solution)/shard_map/ppermute | solution.py:17
  22.7 6.2 %collective-permute-start = (f32[46,1,1024]{2,0,1:T(8,128)S(1)}, f32[46,1,1024]{2,0,1:T(8,128)}, u32[]{:S(2)}, u32[]{:S(2)}) collective-permute-start(f32[46,1,1024]{2,0,1:T(8,128)S(1)} %get-tuple-element.60), channel_id=1, source_target_pairs={{1,0},{2,1},{3,2},{4,3},{5,4},{6,5},{7,6},{8,7},{9,8},{10,9},{11,1... | collective-permute-start | bytes 565256 | tf_op jit(solution)/shard_map/ppermute | solution.py:19
  28.9 1.1 copy.35
  30.1 0.6 dynamic_slice.18
  31.3 2.0 multiply_multiply_fusion
  33.3 1.6 pad_maximum_fusion
  34.9 4.8 %fusion.22 = f32[46,16,1024]{2,0,1:T(8,128)} fusion(f32[46,16,1024]{2,0,1:T(8,128)S(1)} %pad_maximum_fusion, f32[46,1,1024]{2,0,1:T(8,128)} %collective-permute-done.1, f32[40,16,1024]{2,0,1:T(8,128)S(1)} %copy.27, f32[6,16,1024]{2,0,1:T(8,128)S(1)} %copy-done.3, f32[46,1,1024]{2,0,1:T(8,128)} %collective-permute-done), kind=kLoop, calls=%fused_computation.32 | loop fusion | flops 6782976 | bytes 9420800 | tf_op jit(solution)/shard_map/sub | solution.py:70
  39.7 98.6 %all-reduce.3.cloned.1.call-done = f32[16,1024]{1,0:T(8,128)} async-done(((f32[16,1024]{1,0:T(8,128)}), f32[16,1024]{1,0:T(8,128)}) %all-reduce.3.cloned.1.call-update) | async-done | bytes 65552 | tf_op jit(solution)/shard_map/psum | solution.py:65
  138.4 8.8 %fusion.29 = f32[40,16,1024]{2,0,1:T(8,128)S(1)} fusion(f32[46,16,1024]{2,0,1:T(8,128)} %fusion.22, f32[16,1024]{1,0:T(8,128)} %all-reduce.3.cloned.1.call-done, f32[40]{0:T(128)S(1)} %copy-done.10, f32[40]{0:T(128)S(1)} %copy-done.11, f32[40,40]{1,0:T(8,128)S(1)} %copy-done, f32[40,16,1024]{2,1,0:T(8,128)} %param.12, f32[5,8,16,1024]{3,2,1,0:T(8,128)} %bitcast.43), kind=kOutput, calls=%fused_computation.44 | convolution fusion | flops 317849600 | bytes 10558016 | tf_op jit(solution)/shard_map/dot_general | solution.py:72
  147.2 3.0 copy.33
  150.2 102.7 %all-gather.3.cloned.1.call-done = f32[16,6,16384]{2,1,0:T(8,128)} async-done(((f32[1,6,16384]{2,1,0:T(8,128)}), f32[16,6,16384]{2,1,0:T(8,128)}) %all-gather.3.cloned.1.call-update) | async-done | bytes 6291472 | tf_op jit(solution)/shard_map/all_gather | solution.py:51
  253.0 6.6 %reshape.39 = f32[96,16384]{1,0:T(8,128)} reshape(f32[16,6,16384]{2,1,0:T(8,128)} %all-gather.3.cloned.1.call-done) | data formatting | bytes 12582912
  259.6 63.8 %while.10 = (s32[]{:T(128)}, f32[6,16384]{1,0:T(8,128)S(1)}, f32[96,96]{1,0:T(8,128)S(1)}, s32[6]{0:T(128)S(1)}, s32[96,96]{1,0:T(8,128)S(1)}, /*index=5*/f32[96...) while((s32[]{:T(128)}, f32[6,16384]{1,0:T(8,128)S(1)}, f32[96,96]{1,0:T(8,128)S(1)}, ...), condition=%wide.region_2.3_spmd, body=%wide.region_0.2_spmd.sunk | while | flops 1815151616 | bytes 6598777 | solution.py:41
  259.6 0.6 dynamic_slice.24
  260.2 9.5 %fusion.48 = f32[16384]{0:T(1024)S(1)} fusion(f32[96,16384]{1,0:T(8,128)} %get-tuple-element.132, f32[96,96]{1,0:T(8,128)S(1)} %get-tuple-element.131, f32[96,96]{1,0:T(8,128)S(1)} %get-tuple-element.128, s32[96,96]{1,0:T(8,128)S(1)} %get-tuple-element.130, s32[]{:T(128)} %bitcast.41), kind=kOutput, calls=%fused_computation.1.clone.1 | convolution fusion | flops 1815151616 | bytes 6467588 | tf_op jit(solution)/shard_map/while/body/eval_jaxpr/dot_general | solution.py:37
  270.2 0.6 dynamic_slice.24
  270.8 9.5 %fusion.48 = f32[16384]{0:T(1024)S(1)} fusion(f32[96,16384]{1,0:T(8,128)} %get-tuple-element.132, f32[96,96]{1,0:T(8,128)S(1)} %get-tuple-element.131, f32[96,96]{1,0:T(8,128)S(1)} %get-tuple-element.128, s32[96,96]{1,0:T(8,128)S(1)} %get-tuple-element.130, s32[]{:T(128)} %bitcast.41), kind=kOutput, calls=%fused_computation.1.clone.1 | convolution fusion | flops 1815151616 | bytes 6467588 | tf_op jit(solution)/shard_map/while/body/eval_jaxpr/dot_general | solution.py:37
  281.5 9.5 %fusion.48 = f32[16384]{0:T(1024)S(1)} fusion(f32[96,16384]{1,0:T(8,128)} %get-tuple-element.132, f32[96,96]{1,0:T(8,128)S(1)} %get-tuple-element.131, f32[96,96]{1,0:T(8,128)S(1)} %get-tuple-element.128, s32[96,96]{1,0:T(8,128)S(1)} %get-tuple-element.130, s32[]{:T(128)} %bitcast.41), kind=kOutput, calls=%fused_computation.1.clone.1 | convolution fusion | flops 1815151616 | bytes 6467588 | tf_op jit(solution)/shard_map/while/body/eval_jaxpr/dot_general | solution.py:37
  292.1 9.5 %fusion.48 = f32[16384]{0:T(1024)S(1)} fusion(f32[96,16384]{1,0:T(8,128)} %get-tuple-element.132, f32[96,96]{1,0:T(8,128)S(1)} %get-tuple-element.131, f32[96,96]{1,0:T(8,128)S(1)} %get-tuple-element.128, s32[96,96]{1,0:T(8,128)S(1)} %get-tuple-element.130, s32[]{:T(128)} %bitcast.41), kind=kOutput, calls=%fused_computation.1.clone.1 | convolution fusion | flops 1815151616 | bytes 6467588 | tf_op jit(solution)/shard_map/while/body/eval_jaxpr/dot_general | solution.py:37
  302.7 9.5 %fusion.48 = f32[16384]{0:T(1024)S(1)} fusion(f32[96,16384]{1,0:T(8,128)} %get-tuple-element.132, f32[96,96]{1,0:T(8,128)S(1)} %get-tuple-element.131, f32[96,96]{1,0:T(8,128)S(1)} %get-tuple-element.128, s32[96,96]{1,0:T(8,128)S(1)} %get-tuple-element.130, s32[]{:T(128)} %bitcast.41), kind=kOutput, calls=%fused_computation.1.clone.1 | convolution fusion | flops 1815151616 | bytes 6467588 | tf_op jit(solution)/shard_map/while/body/eval_jaxpr/dot_general | solution.py:37
  313.3 9.5 %fusion.48 = f32[16384]{0:T(1024)S(1)} fusion(f32[96,16384]{1,0:T(8,128)} %get-tuple-element.132, f32[96,96]{1,0:T(8,128)S(1)} %get-tuple-element.131, f32[96,96]{1,0:T(8,128)S(1)} %get-tuple-element.128, s32[96,96]{1,0:T(8,128)S(1)} %get-tuple-element.130, s32[]{:T(128)} %bitcast.41), kind=kOutput, calls=%fused_computation.1.clone.1 | convolution fusion | flops 1815151616 | bytes 6467588 | tf_op jit(solution)/shard_map/while/body/eval_jaxpr/dot_general | solution.py:37
  323.4 1.1 multiply_multiply_fusion.1
  324.5 5.1 %fusion.19 = f32[6,16384]{1,0:T(8,128)S(1)} fusion(f32[6,16384]{1,0:T(8,128)S(1)} %get-tuple-element.39, f32[6,16384]{1,0:T(8,128)S(1)} %bitcast.47, f32[96,16384]{1,0:T(8,128)} %get-tuple-element.137, f32[5,16384]{1,0:T(8,128)S(1)} %bitcast.48, f32[1,16384]{1,0:T(1,128)S(1)} %multiply_multiply_fusion.1, f32[16384]{0:T(1024)S(1)} %bitcast.51, ...), kind=kOutput, calls=%fused_computation.22 | convolution fusion | flops 113934336 | bytes 8393220 | tf_op jit(solution)/shard_map/dot_general | solution.py:55
  329.7 1.4 fusion.31
  331.1 1.0 copy.32
  (46 shorter events, 5.6 us)
Async XLA Ops:
  7.2 131.2 %copy-start = (f32[40,40]{1,0:T(8,128)S(1)}, f32[40,40]{1,0:T(8,128)}, u32[]{:S(2)}) copy-start(f32[40,40]{1,0:T(8,128)} %param.18) | copy-start | bytes 19204
  7.2 131.2 %all-reduce.3.cloned.1.call-start = ((), (), s32[]{:S(2)}) async-start(), calls=%async_computation | async-start | bytes 131072 | tf_op jit(solution)/shard_map/psum | solution.py:65
  10.6 242.4 %all-gather.3.cloned.1.call-start = ((), (), s32[]{:S(2)}) async-start(), calls=%async_computation.1 | async-start | bytes 8912896 | tf_op jit(solution)/shard_map/all_gather | solution.py:51
  13.9 4.2 %copy-start.2 = (f32[6,16,1024]{2,0,1:T(8,128)}, f32[6,16,1024]{2,0,1:T(8,128)S(1)}, u32[]{:S(2)}) copy-start(f32[6,16,1024]{2,0,1:T(8,128)S(1)} %copy.28) | copy-start | bytes 1179652
  13.9 15.0 %copy-start.1 = (f32[6,16,1024]{2,1,0:T(8,128)S(1)}, f32[6,16,1024]{2,1,0:T(8,128)}, u32[]{:S(2)}) copy-start(f32[6,16,1024]{2,1,0:T(8,128)} %param.11) | copy-start | bytes 1179652
  17.4 12.7 %copy-start.12 = (f32[96]{0:T(128)S(1)}, f32[96]{0:T(128)}, u32[]{:S(2)}) copy-start(f32[96]{0:T(128)} %param.16) | copy-start | bytes 1156
  18.1 16.7 %collective-permute-start.1 = (f32[46,1,1024]{2,0,1:T(8,128)}, f32[46,1,1024]{2,0,1:T(8,128)}, u32[]{:S(2)}, u32[]{:S(2)}) collective-permute-start(f32[46,1,1024]{2,0,1:T(8,128)} %get-tuple-element.61), channel_id=1, source_target_pairs={{0,1},{1,2},{2,3},{3,4},{4,5},{5,6},{6,7},{7,8},{8,9},{9,10},{10,1... | collective-permute-start | bytes 565256 | tf_op jit(solution)/shard_map/ppermute | solution.py:17
  22.7 12.2 %collective-permute-start = (f32[46,1,1024]{2,0,1:T(8,128)S(1)}, f32[46,1,1024]{2,0,1:T(8,128)}, u32[]{:S(2)}, u32[]{:S(2)}) collective-permute-start(f32[46,1,1024]{2,0,1:T(8,128)S(1)} %get-tuple-element.60), channel_id=1, source_target_pairs={{1,0},{2,1},{3,2},{4,3},{5,4},{6,5},{7,6},{8,7},{9,8},{10,9},{11,1... | collective-permute-start | bytes 565256 | tf_op jit(solution)/shard_map/ppermute | solution.py:19
  33.3 1.6 copy-start.3
  34.8 103.5 %copy-start.10 = (f32[40]{0:T(128)S(1)}, f32[40]{0:T(128)}, u32[]{:S(2)}) copy-start(f32[40]{0:T(128)} %param.19) | copy-start | bytes 484
  34.9 103.5 %copy-start.11 = (f32[40]{0:T(128)S(1)}, f32[40]{0:T(128)}, u32[]{:S(2)}) copy-start(f32[40]{0:T(128)} %param.17) | copy-start | bytes 484
  150.2 109.3 %copy-start.6 = (f32[96,96]{1,0:T(8,128)S(1)}, f32[96,96]{1,0:T(8,128)}, u32[]{:S(2)}) copy-start(f32[96,96]{1,0:T(8,128)} %param.13) | copy-start | bytes 110596
  150.2 109.3 %copy-start.7 = (s32[96,96]{1,0:T(8,128)S(1)}, s32[96,96]{1,0:T(8,128)}, u32[]{:S(2)}) copy-start(s32[96,96]{1,0:T(8,128)} %param.15) | copy-start | bytes 110596
  150.2 109.3 %copy-start.8 = (f32[96,96]{1,0:T(8,128)S(1)}, f32[96,96]{1,0:T(8,128)}, u32[]{:S(2)}) copy-start(f32[96,96]{1,0:T(8,128)} %param.14) | copy-start | bytes 110596
  150.2 109.3 %copy-start.9 = (f32[6,16384]{1,0:T(8,128)S(1)}, f32[6,16384]{1,0:T(8,128)}, u32[]{:S(2)}) copy-start(f32[6,16384]{1,0:T(8,128)} %custom-call) | copy-start | bytes 1179652
  259.6 64.9 %copy-start.4 = (f32[1,6,16,1024]{3,1,2,0:T(8,128)S(1)}, f32[1,6,16,1024]{3,1,2,0:T(8,128)}, u32[]{:S(2)}) copy-start(f32[1,6,16,1024]{3,1,2,0:T(8,128)} %copy.35) | copy-start | bytes 1179652
  259.6 64.9 %copy-start.5 = (f32[6,16384]{1,0:T(8,128)S(1)}, f32[6,16384]{1,0:T(8,128)}, u32[]{:S(2)}) copy-start(f32[6,16384]{1,0:T(8,128)} %multiply_multiply_fusion) | copy-start | bytes 1179652
Sparse Core Ops, SparseCore 0:
  10.9 127.4 all-reduce.2
  140.7 112.2 all-gather.2
where the time goes:
time: 340 us; the launch traced here: 339 us
  waiting for transfers between devices  201 us (59%)
  matrix products  71.1 us (21%)
  local copies, waits for them, and re-layouts  27.2 us (8%)
  between operations  14.9 us (4%)
  other arithmetic  13.3 us (4%)
  starting transfers between devices  10.8 us (3%)
    all_gather x1, waiting for transfers between devices, shards(): whole = lax.all_gather(flat, 'sec', axis=0, tiled=True)  103 us
    psum x1, waiting for transfers between devices, shards(): consumption = lax.psum(jnp.sum(flux, axis=0), 'sec')  98.6 us
    dot_general x6, matrix products, one_target(): product = jnp.dot(weights, dense, precision=HI)  57.1 us
    unnamed x35, local copies, waits for them, and re-layouts  18.5 us
    dot_general x1, matrix products, shards(): jnp.dot(reaction, species.reshape(kinds, cells), precision=HI)  8.83 us
  transfers between devices with their start and end apart: 4, of which 2 were waited for; matrix products, arithmetic and copies ran while one was open for 9% of the time, Pallas kernels for 0%

commit v1 on v0

v1 whole, which is shorter than its diff:
```python
import functools

import jax
import jax.numpy as jnp
from jax import lax
from jax.experimental import pallas as pl
from jax.experimental.pallas import tpu as pltpu
from jax.sharding import PartitionSpec as P

MESH = pl.DeviceIdType.MESH
F32, BF16 = jnp.float32, jnp.bfloat16
PAD = 8
LOW, HIGH = -1, 4
SLOTS = HIGH - LOW + 1


def split_bf16(x):
    high = x.astype(BF16)
    return high, (x - high.astype(F32)).astype(BF16)


def kernel(
    nsec, nxs, own, kinds,
    soot, species, kern, split, target, growth, diffusivity, reaction, stoich,
    soot_out, species_out,
    fields, result, dense, rate, used, rate_in, used_in,
    edge_out, edge_in, kern_v, split_v, target_v, growth_v, diff_v, react_v,
    react_pad, weights, lhs,
    load_sem, send_sem, recv_sem, back_send, back_recv, used_send, used_recv, edge_send, edge_recv,
):
    sections = nsec * own
    count = fields.shape[1]
    rows = fields.shape[2]
    blocks = fields.shape[0]
    width = blocks * 128
    me = lax.axis_index("sec")
    at = lax.axis_index("xs")
    before, after = (at + nxs - 1) % nxs, (at + 1) % nxs

    barrier = pltpu.get_barrier_semaphore()
    for step in range(1, nsec):
        pl.semaphore_signal(barrier, inc=1, device_id={"sec": (me + step) % nsec}, device_id_type=MESH)
    for neighbour in (before, after):
        pl.semaphore_signal(barrier, inc=1, device_id={"xs": neighbour}, device_id_type=MESH)

    def tile_rows(p):
        return pl.ds(pl.multiple_of((p // blocks) * 8, 8), 8)

    def tile_of(ref, p):
        return ref.at[:, tile_rows(p), pl.ds(pl.multiple_of((p % blocks) * 128, 128), 128)]

    loads = [pltpu.make_async_copy(tile_of(soot, me), dense.at[pl.ds(PAD + own * me, own)], load_sem.at[0])]
    for b in range(blocks):
        lanes = pl.ds(b * 128, 128)
        loads.append(pltpu.make_async_copy(species.at[:, :, lanes], fields.at[b, pl.ds(0, kinds)], load_sem.at[1 + b]))
        loads.append(pltpu.make_async_copy(soot.at[:, :, lanes], fields.at[b, pl.ds(kinds, own)], load_sem.at[1 + blocks + b]))
    tables = [(kern, kern_v), (split, split_v), (target, target_v), (growth, growth_v), (diffusivity, diff_v), (reaction, react_v)]
    for n, (src, dst) in enumerate(tables):
        loads.append(pltpu.make_async_copy(src, dst, load_sem.at[1 + 2 * blocks + n]))
    for copy in loads:
        copy.start()

    pl.semaphore_wait(barrier, nsec + 1)

    def sent(p, step):
        return pltpu.make_async_remote_copy(
            src_ref=tile_of(soot, p), dst_ref=dense.at[pl.ds(PAD + own * me, own)],
            send_sem=send_sem.at[step], recv_sem=recv_sem.at[me],
            device_id={"sec": p}, device_id_type=MESH)

    def got(p, step):
        return pltpu.make_async_remote_copy(
            src_ref=tile_of(soot, p), dst_ref=dense.at[pl.ds(PAD + own * p, own)],
            send_sem=send_sem.at[step], recv_sem=recv_sem.at[p],
            device_id={"sec": p}, device_id_type=MESH)

    for step in range(1, nsec):
        sent((me + step) % nsec, step).start()

    zero_tiles = jnp.zeros((PAD, 8, 128), F32)
    dense[0:PAD] = zero_tiles
    dense[PAD + sections:] = zero_tiles
    fields[:, kinds + own:] = jnp.zeros((blocks, count - kinds - own, rows, 128), F32)
    for copy in loads:
        copy.wait()

    flat = fields.reshape(blocks, count * rows, 128)
    flat_result = result.reshape(blocks, count * rows, 128)

    def row_of(r):
        return jnp.concatenate([flat[b, pl.ds(r, count, stride=rows), :] for b in range(blocks)], axis=1)

    edge_out[0] = row_of(0)
    edge_out[1] = row_of(rows - 1)

    def edge(side):
        return pltpu.make_async_remote_copy(
            src_ref=edge_out.at[side], dst_ref=edge_in.at[side],
            send_sem=edge_send.at[side], recv_sem=edge_recv.at[side],
            device_id={"xs": before if side == 0 else after}, device_id_type=MESH)

    edge(0).start()
    edge(1).start()

    i = lax.broadcasted_iota(jnp.int32, (sections, sections), 0)
    j = lax.broadcasted_iota(jnp.int32, (sections, sections), 1)
    rates = kern_v[...]
    shares = split_v[...]
    goal = target_v[...]
    low = 0.5 * rates * shares
    high = 0.5 * rates * (1.0 - shares)
    low_t, high_t, goal_t = low.T, high.T, goal.T
    weights[...] = jnp.zeros(weights.shape, F32)
    for slot in range(SLOTS):
        t = slot + LOW
        lower = jnp.where(goal == i + t, low, 0.0) + jnp.where(goal == i + (t - 1), high, 0.0)
        upper = jnp.where(goal_t == i + t, low_t, 0.0) + jnp.where(goal_t == i + (t - 1), high_t, 0.0)
        value = jnp.where(j <= i, lower, 0.0) + jnp.where(j < i, upper, 0.0)
        if t == 0:
            value = value - rates
        weights[slot, PAD + t:PAD + t + sections, 0:sections] = value
    for slot in range(SLOTS):
        top, rest = split_bf16(weights[slot, PAD:PAD + sections, :])
        here = pl.ds(slot * sections, sections)
        lhs[here, 0:128] = top
        lhs[here, 128:256] = top
        lhs[here, 256:384] = rest
    grow = growth_v[...].reshape(1, sections)
    grow_col = jnp.sum(jnp.where(i == j, grow, 0.0), axis=1, keepdims=True)
    grow_prev = jnp.sum(jnp.where(i == j + 1, grow, 0.0), axis=1, keepdims=True)

    fi = lax.broadcasted_iota(jnp.int32, (count, kinds), 0)
    fj = lax.broadcasted_iota(jnp.int32, (count, kinds), 1)
    diff_col = jnp.sum(jnp.where(fi == fj, diff_v[...].reshape(1, kinds), 0.0), axis=1, keepdims=True)
    fc = lax.broadcasted_iota(jnp.int32, (count, 1), 0)
    diff_col = diff_col + jnp.where((fc >= kinds) & (fc < kinds + own), 0.1, 0.0)
    react_pad[...] = jnp.zeros(react_pad.shape, F32)
    react_pad[0:kinds, 0:kinds] = react_v[...]
    mix = react_pad[...]
    mix_top = mix.astype(BF16).astype(F32)
    mix_rest = mix - mix_top
    mix_lhs = (mix_top + pltpu.roll(mix_top, kinds, 1) + pltpu.roll(mix_rest, 2 * kinds, 1)).astype(BF16)
    lane = lax.broadcasted_iota(jnp.int32, (count, width), 1)
    spare = jnp.zeros((128 - 3 * kinds, width), F32)

    def row_step(r, up, down):
        x = row_of(r)
        left = jnp.where(lane == 0, 0.0, pltpu.roll(x, 1, 1))
        right = jnp.where(lane == width - 1, 0.0, pltpu.roll(x, width - 1, 1))
        part = x[0:kinds]
        top = part.astype(BF16).astype(F32)
        rhs = jnp.concatenate([top, part - top, top, spare], axis=0).astype(BF16)
        mixed = jnp.dot(mix_lhs, rhs, preferred_element_type=F32)
        value = x + diff_col * (up + down + left + right - 4.0 * x) + mixed
        for b in range(blocks):
            flat_result[b, pl.ds(r, count, stride=rows), :] = value[:, b * 128:(b + 1) * 128]

    def inner(r, carry):
        row_step(r, row_of(r - 1), row_of(r + 1))
        return carry

    half = rows // 2
    lax.fori_loop(1, half, inner, 0)

    for step in range(1, nsec):
        got((me + step) % nsec, step).wait_recv()

    flat_dense = dense.reshape((sections + 2 * PAD) * 8, 128)
    flat_rate = rate.reshape(sections * 8, 128)
    acet = fields[me % blocks, 0, tile_rows(me), :]
    gap = jnp.zeros((128 - sections, 256), BF16)
    for pair in range(4):
        r0, r1 = 2 * pair, 2 * pair + 1

        def moved(t):
            start = 8 * (PAD - t)
            return jnp.concatenate(
                [flat_dense[pl.ds(start + r, sections, stride=8), :] for r in (r0, r1)], axis=1)

        held = moved(0)
        top, rest = split_bf16(held)
        rhs = jnp.concatenate([top, gap, rest, gap], axis=0)
        product = jnp.dot(lhs[:, 0:256], rhs, preferred_element_type=F32)
        product = product + jnp.dot(lhs[:, 256:384], rhs[0:128], preferred_element_type=F32)
        total = jnp.zeros((sections, 256), F32)
        for slot in range(SLOTS):
            total = total + moved(slot + LOW) * product[slot * sections:(slot + 1) * sections]
        growing = jnp.concatenate([acet[r0:r0 + 1], acet[r1:r1 + 1]], axis=1)
        flux = grow_col * held * growing
        total = total - flux + grow_prev * moved(1) * growing
        eaten = jnp.sum(flux, axis=0, keepdims=True)
        for n, r in enumerate((r0, r1)):
            flat_rate[pl.ds(r, sections, stride=8), :] = total[:, n * 128:(n + 1) * 128]
            used[r:r + 1, :] = eaten[:, n * 128:(n + 1) * 128]

    def rate_copy(p, source, step):
        return pltpu.make_async_remote_copy(
            src_ref=rate.at[pl.ds(own * p, own)], dst_ref=rate_in.at[source % blocks, :, tile_rows(source), :],
            send_sem=back_send.at[step], recv_sem=back_recv.at[source],
            device_id={"sec": p}, device_id_type=MESH)

    def used_copy(p, source, step):
        return pltpu.make_async_remote_copy(
            src_ref=used, dst_ref=used_in.at[source % blocks, tile_rows(source), :],
            send_sem=used_send.at[step], recv_sem=used_recv.at[source],
            device_id={"sec": p}, device_id_type=MESH)

    for step in range(1, nsec):
        p = (me + step) % nsec
        rate_copy(p, me, step).start()
        used_copy(p, me, step).start()
    rate_in[me % blocks, :, tile_rows(me), :] = rate[pl.ds(own * me, own)]
    used_in[me % blocks, tile_rows(me), :] = used[...]

    lax.fori_loop(half, rows - 1, inner, 0)
    edge(0).wait()
    edge(1).wait()
    row_step(0, jnp.where(at == 0, 0.0, edge_in[1]), row_of(1))
    row_step(rows - 1, row_of(rows - 2), jnp.where(at == nxs - 1, 0.0, edge_in[0]))

    for step in range(1, nsec):
        p = (me + step) % nsec
        rate_copy(p, p, step).wait_recv()
        used_copy(p, p, step).wait_recv()

    result[:, kinds:kinds + own] = result[:, kinds:kinds + own] + rate_in[...]

    def consume(s, carry):
        result[:, s] = result[:, s] - stoich[s] * used_in[...]
        return carry

    lax.fori_loop(0, kinds, consume, 0)

    stores = []
    for b in range(blocks):
        lanes = pl.ds(b * 128, 128)
        stores.append(pltpu.make_async_copy(result.at[b, pl.ds(0, kinds)], species_out.at[:, :, lanes], load_sem.at[1 + b]))
        stores.append(pltpu.make_async_copy(result.at[b, pl.ds(kinds, own)], soot_out.at[:, :, lanes], load_sem.at[1 + blocks + b]))
    for copy in stores:
        copy.start()
    for step in range(1, nsec):
        p = (me + step) % nsec
        sent(p, step).wait_send()
        rate_copy(p, me, step).wait_send()
        used_copy(p, me, step).wait_send()
    for copy in stores:
        copy.wait()


def shards(soot, species, kern, split, target, growth, diffusivity, reaction, stoich):
    own, rows, width = soot.shape
    kinds = species.shape[0]
    nsec, nxs = lax.axis_size("sec"), lax.axis_size("xs")
    sections = nsec * own
    blocks = width // 128
    count = -(-(kinds + own) // 8) * 8
    assert blocks * (rows // 8) == nsec and sections <= 128 and 3 * kinds <= 128
    dma = pltpu.SemaphoreType.DMA
    hbm = pl.BlockSpec(memory_space=pl.ANY)
    return pl.pallas_call(
        functools.partial(kernel, nsec, nxs, own, kinds),
        out_shape=(jax.ShapeDtypeStruct(soot.shape, F32), jax.ShapeDtypeStruct(species.shape, F32)),
        in_specs=[hbm] * 8 + [pl.BlockSpec(memory_space=pltpu.SMEM)],
        out_specs=(hbm, hbm),
        scratch_shapes=[
            pltpu.VMEM((blocks, count, rows, 128), F32),
            pltpu.VMEM((blocks, count, rows, 128), F32),
            pltpu.VMEM((sections + 2 * PAD, 8, 128), F32),
            pltpu.VMEM((sections, 8, 128), F32),
            pltpu.VMEM((8, 128), F32),
            pltpu.VMEM((blocks, own, rows, 128), F32),
            pltpu.VMEM((blocks, rows, 128), F32),
            pltpu.VMEM((2, count, width), F32),
            pltpu.VMEM((2, count, width), F32),
            pltpu.VMEM(kern.shape, F32),
            pltpu.VMEM(split.shape, F32),
            pltpu.VMEM(target.shape, jnp.int32),
            pltpu.VMEM(growth.shape, F32),
            pltpu.VMEM(diffusivity.shape, F32),
            pltpu.VMEM(reaction.shape, F32),
            pltpu.VMEM((count, 128), F32),
            pltpu.VMEM((SLOTS, sections + 2 * PAD, 128), F32),
            pltpu.VMEM((SLOTS * sections, 384), BF16),
            dma((1 + 2 * blocks + 6,)),
            dma((nsec,)), dma((nsec,)), dma((nsec,)), dma((nsec,)), dma((nsec,)), dma((nsec,)),
            dma((2,)), dma((2,)),
        ],
        compiler_params=pltpu.CompilerParams(
            collective_id=0, has_side_effects=True, vmem_limit_bytes=32 << 20),
    )(soot, species, kern, split, target, growth, diffusivity, reaction, stoich)


def solution(mesh):
    return jax.shard_map(
        shards,
        mesh=mesh,
        in_specs=(P("sec", "xs", None), P(None, "xs", None), P(), P(), P(), P(), P(), P(), P()),
        out_specs=(P("sec", "xs", None), P(None, "xs", None)),
        check_vma=False,
    )
```

time: 340 us -> 49.2 us (0.14)
  the two profiles are of different devices: /device:TPU:1 before, /device:TPU:16 now
where the time goes in v1:
time: 49.2 us; the launch traced here: 48.7 us
  Pallas kernels  38 us (77%)
  local copies, waits for them, and re-layouts  10.1 us (21%)
  between operations  0.66 us (1%)
    pallas_call x1, Pallas kernels, shards(): pl.pallas_call(functools.partial(kernel, nsec, nxs, own, kinds), out_shap...  38 us
    unnamed x20, local copies, waits for them, and re-layouts  10.1 us

profile of v1, /device:TPU:16, one launch (start us, length us, event | category | flops | bytes accessed | tf_op | source)
XLA Modules:
  0.0 48.7 jit_solution(14775112115471602568)
XLA Ops:
  0.6 0.0 copy-start
  0.6 1.7 %copy-done = f32[40,16,1024]{2,1,0:T(8,128)S(1)} copy-done((f32[40,16,1024]{2,1,0:T(8,128)S(1)}, f32[40,16,1024]{2,1,0:T(8,128)}, u32[]{:S(2)}) %copy-start) | copy-done | bytes 2621464
  2.4 0.0 copy-start.1
  2.4 1.0 %copy-done.1 = f32[6,16,1024]{2,1,0:T(8,128)S(1)} copy-done((f32[6,16,1024]{2,1,0:T(8,128)S(1)}, f32[6,16,1024]{2,1,0:T(8,128)}, u32[]{:S(2)}) %copy-start.1) | copy-done | bytes 393240
  3.4 0.0 copy-start.2
  3.4 0.8 %copy-done.2 = f32[96,96]{1,0:T(8,128)S(1)} copy-done((f32[96,96]{1,0:T(8,128)S(1)}, f32[96,96]{1,0:T(8,128)}, u32[]{:S(2)}) %copy-start.2) | copy-done | bytes 36888
  4.2 0.0 copy-start.3
  4.2 0.8 %copy-done.3 = f32[96,96]{1,0:T(8,128)S(1)} copy-done((f32[96,96]{1,0:T(8,128)S(1)}, f32[96,96]{1,0:T(8,128)}, u32[]{:S(2)}) %copy-start.3) | copy-done | bytes 36888
  5.0 0.0 copy-start.4
  5.0 0.8 %copy-done.4 = s32[96,96]{1,0:T(8,128)S(1)} copy-done((s32[96,96]{1,0:T(8,128)S(1)}, s32[96,96]{1,0:T(8,128)}, u32[]{:S(2)}) %copy-start.4) | copy-done | bytes 36888
  5.8 0.0 copy-start.5
  5.8 0.7 %copy-done.5 = f32[40,40]{1,0:T(8,128)S(1)} copy-done((f32[40,40]{1,0:T(8,128)S(1)}, f32[40,40]{1,0:T(8,128)}, u32[]{:S(2)}) %copy-start.5) | copy-done | bytes 6424
  6.5 0.0 copy-start.6
  6.5 0.7 %copy-done.6 = f32[96]{0:T(128)S(1)} copy-done((f32[96]{0:T(128)S(1)}, f32[96]{0:T(128)}, u32[]{:S(2)}) %copy-start.6) | copy-done | bytes 408
  7.2 0.0 copy-start.7
  7.2 0.7 %copy-done.7 = f32[40]{0:T(128)S(1)} copy-done((f32[40]{0:T(128)S(1)}, f32[40]{0:T(128)}, u32[]{:S(2)}) %copy-start.7) | copy-done | bytes 184
  7.8 0.0 copy-start.8
  7.8 0.7 %copy-done.8 = f32[40]{0:T(128)S(1)} copy-done((f32[40]{0:T(128)S(1)}, f32[40]{0:T(128)}, u32[]{:S(2)}) %copy-start.8) | copy-done | bytes 184
  8.5 38.0 %shard_map.104 = (f32[6,16,1024]{2,1,0:T(8,128)S(1)}, f32[40,16,1024]{2,1,0:T(8,128)S(1)}) custom-call(f32[6,16,1024]{2,1,0:T(8,128)S(1)} %copy-done.1, f32[40,16,1024]{2,1,0:T(8,128)S(1)} %copy-done, f32[96,96]{1,0:T(8,128)S(1)} %copy-done.2, f32[96,96]{1,0:T(8,128)S(1)} %copy-done.3, s32[96,96]{1,0:T(8,128)S(1)} %copy-done.4, f32[96]{0:T(128)S(1)} %copy-done.6, ...), custom_call_target="tpu_custom_call" | custom-call | tf_op jit(solution)/shard_map/pallas_call | solution.py:260
  46.5 0.7 %copy.13 = f32[6,16,1024]{2,1,0:T(8,128)} copy(f32[6,16,1024]{2,1,0:T(8,128)S(1)} %get-tuple-element.4) | data formatting | bytes 786432
  47.2 1.5 %copy.14 = f32[40,16,1024]{2,1,0:T(8,128)} copy(f32[40,16,1024]{2,1,0:T(8,128)S(1)} %get-tuple-element.5) | data formatting | bytes 5242880
Async XLA Ops:
  0.6 1.7 %copy-start = (f32[40,16,1024]{2,1,0:T(8,128)S(1)}, f32[40,16,1024]{2,1,0:T(8,128)}, u32[]{:S(2)}) copy-start(f32[40,16,1024]{2,1,0:T(8,128)} %species.1) | copy-start | bytes 7864324
  2.4 1.0 %copy-start.1 = (f32[6,16,1024]{2,1,0:T(8,128)S(1)}, f32[6,16,1024]{2,1,0:T(8,128)}, u32[]{:S(2)}) copy-start(f32[6,16,1024]{2,1,0:T(8,128)} %soot.1) | copy-start | bytes 1179652
  3.4 0.8 %copy-start.2 = (f32[96,96]{1,0:T(8,128)S(1)}, f32[96,96]{1,0:T(8,128)}, u32[]{:S(2)}) copy-start(f32[96,96]{1,0:T(8,128)} %kern.1) | copy-start | bytes 110596
  4.2 0.8 %copy-start.3 = (f32[96,96]{1,0:T(8,128)S(1)}, f32[96,96]{1,0:T(8,128)}, u32[]{:S(2)}) copy-start(f32[96,96]{1,0:T(8,128)} %split.1) | copy-start | bytes 110596
  5.0 0.8 %copy-start.4 = (s32[96,96]{1,0:T(8,128)S(1)}, s32[96,96]{1,0:T(8,128)}, u32[]{:S(2)}) copy-start(s32[96,96]{1,0:T(8,128)} %target.1) | copy-start | bytes 110596
  5.8 0.7 %copy-start.5 = (f32[40,40]{1,0:T(8,128)S(1)}, f32[40,40]{1,0:T(8,128)}, u32[]{:S(2)}) copy-start(f32[40,40]{1,0:T(8,128)} %reaction.1) | copy-start | bytes 19204
  6.5 0.7 %copy-start.6 = (f32[96]{0:T(128)S(1)}, f32[96]{0:T(128)}, u32[]{:S(2)}) copy-start(f32[96]{0:T(128)} %growth.1) | copy-start | bytes 1156
  7.2 0.7 %copy-start.7 = (f32[40]{0:T(128)S(1)}, f32[40]{0:T(128)}, u32[]{:S(2)}) copy-start(f32[40]{0:T(128)} %diffusivity.1) | copy-start | bytes 484
  7.8 0.7 %copy-start.8 = (f32[40]{0:T(128)S(1)}, f32[40]{0:T(128)}, u32[]{:S(2)}) copy-start(f32[40]{0:T(128)} %stoich.1) | copy-start | bytes 484

commit v2 on v1

--- a/solution.py
+++ b/solution.py
@@ -21,9 +21,9 @@
 
 def kernel(
     nsec, nxs, own, kinds,
-    soot, species, kern, split, target, growth, diffusivity, reaction, stoich,
-    soot_out, species_out,
-    fields, result, dense, rate, used, rate_in, used_in,
+    soot, species, kern, split, target, growth, diffusivity, reaction,
+    result, rate_in, used_in,
+    fields, dense, rate, used,
     edge_out, edge_in, kern_v, split_v, target_v, growth_v, diff_v, react_v,
     react_pad, weights, lhs,
     load_sem, send_sem, recv_sem, back_send, back_recv, used_send, used_recv, edge_send, edge_recv,
@@ -223,28 +223,35 @@
         rate_copy(p, p, step).wait_recv()
         used_copy(p, p, step).wait_recv()
 
-    result[:, kinds:kinds + own] = result[:, kinds:kinds + own] + rate_in[...]
-
-    def consume(s, carry):
-        result[:, s] = result[:, s] - stoich[s] * used_in[...]
-        return carry
-
-    lax.fori_loop(0, kinds, consume, 0)
-
-    stores = []
-    for b in range(blocks):
-        lanes = pl.ds(b * 128, 128)
-        stores.append(pltpu.make_async_copy(result.at[b, pl.ds(0, kinds)], species_out.at[:, :, lanes], load_sem.at[1 + b]))
-        stores.append(pltpu.make_async_copy(result.at[b, pl.ds(kinds, own)], soot_out.at[:, :, lanes], load_sem.at[1 + blocks + b]))
-    for copy in stores:
-        copy.start()
     for step in range(1, nsec):
         p = (me + step) % nsec
         sent(p, step).wait_send()
         rate_copy(p, me, step).wait_send()
         used_copy(p, me, step).wait_send()
+
+
+def finish(own, kinds, result, rate_in, used_in, stoich, soot_out, species_out, done, stoich_s, sem, small):
+    blocks = result.shape[0]
+    fetch = pltpu.make_async_copy(stoich, stoich_s, small)
+    fetch.start()
+    fetch.wait()
+    stores = []
+    for b in range(blocks):
+        lanes = pl.ds(b * 128, 128)
+        done[b, kinds:kinds + own] = result[b, kinds:kinds + own] + rate_in[b]
+        used = used_in[b]
+        for s in range(kinds):
+            done[b, s] = result[b, s] - stoich_s[s] * used
+        stores.append(pltpu.make_async_copy(done.at[b, pl.ds(0, kinds)], species_out.at[:, :, lanes], sem.at[b]))
+        stores.append(pltpu.make_async_copy(done.at[b, pl.ds(kinds, own)], soot_out.at[:, :, lanes], sem.at[blocks + b]))
+        stores[-2].start()
+        stores[-1].start()
     for copy in stores:
         copy.wait()
+
+
+def stay(x):
+    return pltpu.with_memory_space_constraint(x, pltpu.HBM)
 
 
 def shards(soot, species, kern, split, target, growth, diffusivity, reaction, stoich):
@@ -256,20 +263,22 @@
     count = -(-(kinds + own) // 8) * 8
     assert blocks * (rows // 8) == nsec and sections <= 128 and 3 * kinds <= 128
     dma = pltpu.SemaphoreType.DMA
-    hbm = pl.BlockSpec(memory_space=pl.ANY)
-    return pl.pallas_call(
+    hbm = pl.BlockSpec(memory_space=pltpu.HBM)
+    vmem = pl.BlockSpec(memory_space=pltpu.VMEM)
+    parts = pl.pallas_call(
         functools.partial(kernel, nsec, nxs, own, kinds),
-        out_shape=(jax.ShapeDtypeStruct(soot.shape, F32), jax.ShapeDtypeStruct(species.shape, F32)),
-        in_specs=[hbm] * 8 + [pl.BlockSpec(memory_space=pltpu.SMEM)],
-        out_specs=(hbm, hbm),
+        out_shape=(
+            jax.ShapeDtypeStruct((blocks, count, rows, 128), F32),
+            jax.ShapeDtypeStruct((blocks, own, rows, 128), F32),
+            jax.ShapeDtypeStruct((blocks, rows, 128), F32),
+        ),
+        in_specs=[hbm] * 8,
+        out_specs=(vmem, vmem, vmem),
         scratch_shapes=[
-            pltpu.VMEM((blocks, count, rows, 128), F32),
             pltpu.VMEM((blocks, count, rows, 128), F32),
             pltpu.VMEM((sections + 2 * PAD, 8, 128), F32),
             pltpu.VMEM((sections, 8, 128), F32),
             pltpu.VMEM((8, 128), F32),
-            pltpu.VMEM((blocks, own, rows, 128), F32),
-            pltpu.VMEM((blocks, rows, 128), F32),
             pltpu.VMEM((2, count, width), F32),
             pltpu.VMEM((2, count, width), F32),
             pltpu.VMEM(kern.shape, F32),
@@ -287,7 +296,20 @@
         ],
         compiler_params=pltpu.CompilerParams(
             collective_id=0, has_side_effects=True, vmem_limit_bytes=32 << 20),
-    )(soot, species, kern, split, target, growth, diffusivity, reaction, stoich)
+    )(*(stay(x) for x in (soot, species, kern, split, target, growth, diffusivity, reaction)))
+    return pl.pallas_call(
+        functools.partial(finish, own, kinds),
+        out_shape=(jax.ShapeDtypeStruct(soot.shape, F32), jax.ShapeDtypeStruct(species.shape, F32)),
+        in_specs=[vmem, vmem, vmem, hbm],
+        out_specs=(hbm, hbm),
+        scratch_shapes=[
+            pltpu.VMEM((blocks, count, rows, 128), F32),
+            pltpu.SMEM(stoich.shape, F32),
+            dma((2 * blocks,)),
+            dma(()),
+        ],
+        compiler_params=pltpu.CompilerParams(vmem_limit_bytes=16 << 20),
+    )(*parts, stay(stoich))
 
 
 def solution(mesh):

time: 49.2 us -> 40 us (0.81)
  local copies, waits for them, and re-layouts: 10.1 us -> 0 us
  Pallas kernels: 38 us -> 39.2 us
    unnamed x20 -> x0, local copies, waits for them, and re-layouts: 10.1 us -> none
    pallas_call x0 -> x1, Pallas kernels: none -> 2.44 us  [shards(): pl.pallas_call(functools.partial(finish, own, kinds), out_shape=(jax.Shap...]
    pallas_call x1, Pallas kernels: 38 us -> 36.8 us  [shards(): pl.pallas_call(functools.partial(kernel, nsec, nxs, own, kinds), out_shap...]
where the time goes in v2:
time: 40 us; the launch traced here: 39.8 us
  Pallas kernels  39.2 us (98%)
  between operations  0.64 us (2%)
    pallas_call x1, Pallas kernels, shards(): pl.pallas_call(functools.partial(kernel, nsec, nxs, own, kinds), out_shap...  36.8 us
    pallas_call x1, Pallas kernels, shards(): pl.pallas_call(functools.partial(finish, own, kinds), out_shape=(jax.Shap...  2.44 us

profile of v2, /device:TPU:16, one launch (start us, length us, event | category | flops | bytes accessed | tf_op | source)
XLA Modules:
  0.0 39.8 jit_solution(11262817585365450988)
XLA Ops:
  0.6 36.8 %shard_map.104 = (f32[8,48,16,128]{3,2,1,0:T(8,128)S(1)}, f32[8,6,16,128]{3,2,1,0:T(8,128)S(1)}, f32[8,16,128]{2,1,0:T(8,128)S(1)}) custom-call(f32[6,16,1024]{2,1,0:T(8,128)} %soot.1, f32[40,16,1024]{2,1,0:T(8,128)} %species.1, f32[96,96]{1,0:T(8,128)} %kern.1, f32[96,96]{1,0:T(8,128)} %split.1, s32[96,96]{1,0:T(8,128)} %target.1, f32[96]{0:T(128)} %growth.1, ...), custom_call_target="tpu_custom_call" | custom-call | tf_op jit(solution)/shard_map/pallas_call | solution.py:268
  37.4 2.4 %shard_map.105 = (f32[6,16,1024]{2,1,0:T(8,128)}, f32[40,16,1024]{2,1,0:T(8,128)}) custom-call(f32[8,48,16,128]{3,2,1,0:T(8,128)S(1)} %get-tuple-element.5.result, f32[8,6,16,128]{3,2,1,0:T(8,128)S(1)} %get-tuple-element.6.rate_in, f32[8,16,128]{2,1,0:T(8,128)S(1)} %get-tuple-element.7.used_in, f32[40]{0:T(128)} %stoich.1), custom_call_target="tpu_custom_call" | custom-call | tf_op jit(solution)/shard_map/pallas_call | solution.py:300

commit v3 on v1

--- a/solution.py
+++ b/solution.py
@@ -10,6 +10,10 @@
 MESH = pl.DeviceIdType.MESH
 F32, BF16 = jnp.float32, jnp.bfloat16
 PAD = 8
+PART = 4
+PARTS = 8 // PART
+ROWS_BEFORE = (5, 10)
+ORDER = (3, 13, 11, 5, 4, 12, 2, 14, 10, 6, 1, 15, 9, 7, 8)
 LOW, HIGH = -1, 4
 SLOTS = HIGH - LOW + 1
 
@@ -22,11 +26,11 @@
 def kernel(
     nsec, nxs, own, kinds,
     soot, species, kern, split, target, growth, diffusivity, reaction, stoich,
-    soot_out, species_out,
-    fields, result, dense, rate, used, rate_in, used_in,
-    edge_out, edge_in, kern_v, split_v, target_v, growth_v, diff_v, react_v,
+    result,
+    fields, dense, rate, used, rate_in, used_in,
+    edge_out, edge_in, kern_v, split_v, target_v, growth_v, diff_v, react_v, stoich_s,
     react_pad, weights, lhs,
-    load_sem, send_sem, recv_sem, back_send, back_recv, used_send, used_recv, edge_send, edge_recv,
+    load_sem, send_sem, recv_sem, back_send, back_recv, used_send, used_recv, edge_send, edge_recv, ready,
 ):
     sections = nsec * own
     count = fields.shape[1]
@@ -40,42 +44,51 @@
     barrier = pltpu.get_barrier_semaphore()
     for step in range(1, nsec):
         pl.semaphore_signal(barrier, inc=1, device_id={"sec": (me + step) % nsec}, device_id_type=MESH)
-    for neighbour in (before, after):
-        pl.semaphore_signal(barrier, inc=1, device_id={"xs": neighbour}, device_id_type=MESH)
+
+    @pl.when(at < nxs - 1)
+    def _():
+        pl.semaphore_signal(barrier, inc=1, device_id={"xs": after}, device_id_type=MESH)
+
 
     def tile_rows(p):
         return pl.ds(pl.multiple_of((p // blocks) * 8, 8), 8)
 
-    def tile_of(ref, p):
-        return ref.at[:, tile_rows(p), pl.ds(pl.multiple_of((p % blocks) * 128, 128), 128)]
-
-    loads = [pltpu.make_async_copy(tile_of(soot, me), dense.at[pl.ds(PAD + own * me, own)], load_sem.at[0])]
+    def part_rows(p, part):
+        return pl.ds(pl.multiple_of((p // blocks) * 8 + part * PART, PART), PART)
+
+    def lanes_of(p):
+        return pl.ds(pl.multiple_of((p % blocks) * 128, 128), 128)
+
+    loads = [pltpu.make_async_copy(soot.at[:, tile_rows(me), lanes_of(me)], dense.at[pl.ds(PAD + own * me, own)], load_sem.at[0])]
     for b in range(blocks):
         lanes = pl.ds(b * 128, 128)
         loads.append(pltpu.make_async_copy(species.at[:, :, lanes], fields.at[b, pl.ds(0, kinds)], load_sem.at[1 + b]))
         loads.append(pltpu.make_async_copy(soot.at[:, :, lanes], fields.at[b, pl.ds(kinds, own)], load_sem.at[1 + blocks + b]))
-    tables = [(kern, kern_v), (split, split_v), (target, target_v), (growth, growth_v), (diffusivity, diff_v), (reaction, react_v)]
+    tables = [(kern, kern_v), (split, split_v), (target, target_v), (growth, growth_v), (diffusivity, diff_v), (reaction, react_v), (stoich, stoich_s)]
     for n, (src, dst) in enumerate(tables):
         loads.append(pltpu.make_async_copy(src, dst, load_sem.at[1 + 2 * blocks + n]))
     for copy in loads:
         copy.start()
 
-    pl.semaphore_wait(barrier, nsec + 1)
-
-    def sent(p, step):
+    @pl.when(at == 0)
+    def _():
+        pl.semaphore_wait(barrier, nsec - 1)
+
+    @pl.when(at > 0)
+    def _():
+        pl.semaphore_wait(barrier, nsec)
+        pl.semaphore_signal(ready, inc=1, device_id={"xs": before}, device_id_type=MESH)
+
+    def cells(p, source, step, part):
         return pltpu.make_async_remote_copy(
-            src_ref=tile_of(soot, p), dst_ref=dense.at[pl.ds(PAD + own * me, own)],
-            send_sem=send_sem.at[step], recv_sem=recv_sem.at[me],
+            src_ref=soot.at[:, part_rows(p, part), lanes_of(p)],
+            dst_ref=dense.at[pl.ds(PAD + own * source, own), pl.ds(part * PART, PART)],
+            send_sem=send_sem.at[part, step], recv_sem=recv_sem.at[part, source],
             device_id={"sec": p}, device_id_type=MESH)
 
-    def got(p, step):
-        return pltpu.make_async_remote_copy(
-            src_ref=tile_of(soot, p), dst_ref=dense.at[pl.ds(PAD + own * p, own)],
-            send_sem=send_sem.at[step], recv_sem=recv_sem.at[p],
-            device_id={"sec": p}, device_id_type=MESH)
-
-    for step in range(1, nsec):
-        sent((me + step) % nsec, step).start()
+    for part in range(PARTS):
+        for step in ORDER:
+            cells((me + step) % nsec, me, step, part).start()
 
     zero_tiles = jnp.zeros((PAD, 8, 128), F32)
     dense[0:PAD] = zero_tiles
@@ -99,8 +112,17 @@
             send_sem=edge_send.at[side], recv_sem=edge_recv.at[side],
             device_id={"xs": before if side == 0 else after}, device_id_type=MESH)
 
-    edge(0).start()
-    edge(1).start()
+    @pl.when(at > 0)
+    def _():
+        edge(0).start()
+
+    @pl.when(at == 0)
+    def _():
+        edge_in[1] = jnp.zeros((count, width), F32)
+
+    @pl.when(at == nxs - 1)
+    def _():
+        edge_in[0] = jnp.zeros((count, width), F32)
 
     i = lax.broadcasted_iota(jnp.int32, (sections, sections), 0)
     j = lax.broadcasted_iota(jnp.int32, (sections, sections), 1)
@@ -159,17 +181,12 @@
         row_step(r, row_of(r - 1), row_of(r + 1))
         return carry
 
-    half = rows // 2
-    lax.fori_loop(1, half, inner, 0)
-
-    for step in range(1, nsec):
-        got((me + step) % nsec, step).wait_recv()
-
     flat_dense = dense.reshape((sections + 2 * PAD) * 8, 128)
     flat_rate = rate.reshape(sections * 8, 128)
     acet = fields[me % blocks, 0, tile_rows(me), :]
     gap = jnp.zeros((128 - sections, 256), BF16)
-    for pair in range(4):
+
+    def rate_pair(pair):
         r0, r1 = 2 * pair, 2 * pair + 1
 
         def moved(t):
@@ -193,58 +210,95 @@
             flat_rate[pl.ds(r, sections, stride=8), :] = total[:, n * 128:(n + 1) * 128]
             used[r:r + 1, :] = eaten[:, n * 128:(n + 1) * 128]
 
-    def rate_copy(p, source, step):
+    def rate_copy(p, source, step, part):
         return pltpu.make_async_remote_copy(
-            src_ref=rate.at[pl.ds(own * p, own)], dst_ref=rate_in.at[source % blocks, :, tile_rows(source), :],
-            send_sem=back_send.at[step], recv_sem=back_recv.at[source],
+            src_ref=rate.at[pl.ds(own * p, own), pl.ds(part * PART, PART)],
+            dst_ref=rate_in.at[source % blocks, :, part_rows(source, part), :],
+            send_sem=back_send.at[part, step], recv_sem=back_recv.at[part, source],
             device_id={"sec": p}, device_id_type=MESH)
 
-    def used_copy(p, source, step):
+    def used_copy(p, source, step, part):
         return pltpu.make_async_remote_copy(
-            src_ref=used, dst_ref=used_in.at[source % blocks, tile_rows(source), :],
-            send_sem=used_send.at[step], recv_sem=used_recv.at[source],
+            src_ref=used.at[pl.ds(part * PART, PART)],
+            dst_ref=used_in.at[source % blocks, part_rows(source, part), :],
+            send_sem=used_send.at[part, step], recv_sem=used_recv.at[part, source],
             device_id={"sec": p}, device_id_type=MESH)
 
-    for step in range(1, nsec):
-        p = (me + step) % nsec
-        rate_copy(p, me, step).start()
-        used_copy(p, me, step).start()
+    first = 1
+    for part in range(PARTS):
+        last = ROWS_BEFORE[part]
+        lax.fori_loop(first, last, inner, 0)
+        first = last
+        for step in range(1, nsec):
+            p = (me + step) % nsec
+            cells(p, p, step, part).wait_recv()
+        for pair in range(part * PART // 2, (part + 1) * PART // 2):
+            rate_pair(pair)
+        for step in ORDER:
+            used_copy((me + step) % nsec, me, step, part).start()
+        for step in ORDER:
+            rate_copy((me + step) % nsec, me, step, part).start()
+        if part == 0:
+            @pl.when(at < nxs - 1)
+            def _():
+                pl.semaphore_wait(ready, 1)
+                edge(1).start()
     rate_in[me % blocks, :, tile_rows(me), :] = rate[pl.ds(own * me, own)]
     used_in[me % blocks, tile_rows(me), :] = used[...]
 
-    lax.fori_loop(half, rows - 1, inner, 0)
-    edge(0).wait()
-    edge(1).wait()
-    row_step(0, jnp.where(at == 0, 0.0, edge_in[1]), row_of(1))
-    row_step(rows - 1, row_of(rows - 2), jnp.where(at == nxs - 1, 0.0, edge_in[0]))
-
-    for step in range(1, nsec):
-        p = (me + step) % nsec
-        rate_copy(p, p, step).wait_recv()
-        used_copy(p, p, step).wait_recv()
-
+    lax.fori_loop(first, rows - 1, inner, 0)
+
+    @pl.when(at > 0)
+    def _():
+        edge(0).wait_send()
+        edge(1).wait_recv()
+
+    @pl.when(at < nxs - 1)
+    def _():
+        edge(1).wait_send()
+        edge(0).wait_recv()
+
+    row_step(0, edge_in[1], row_of(1))
+    row_step(rows - 1, row_of(rows - 2), edge_in[0])
+
+    for part in range(PARTS):
+        for step in range(1, nsec):
+            p = (me + step) % nsec
+            used_copy(p, p, step, part).wait_recv()
+
+    def consume(s, carry):
+        result[:, s] = result[:, s] - stoich_s[s] * used_in[...]
+        return carry
+
+    lax.fori_loop(0, kinds, consume, 0)
+    for part in range(PARTS):
+        for step in range(1, nsec):
+            p = (me + step) % nsec
+            rate_copy(p, p, step, part).wait_recv()
     result[:, kinds:kinds + own] = result[:, kinds:kinds + own] + rate_in[...]
-
-    def consume(s, carry):
-        result[:, s] = result[:, s] - stoich[s] * used_in[...]
-        return carry
-
-    lax.fori_loop(0, kinds, consume, 0)
-
+    for part in range(PARTS):
+        for step in range(1, nsec):
+            p = (me + step) % nsec
+            cells(p, me, step, part).wait_send()
+            rate_copy(p, me, step, part).wait_send()
+            used_copy(p, me, step, part).wait_send()
+
+
+def write_out(own, kinds, result, soot_out, species_out, sem):
+    blocks = result.shape[0]
     stores = []
     for b in range(blocks):
         lanes = pl.ds(b * 128, 128)
-        stores.append(pltpu.make_async_copy(result.at[b, pl.ds(0, kinds)], species_out.at[:, :, lanes], load_sem.at[1 + b]))
-        stores.append(pltpu.make_async_copy(result.at[b, pl.ds(kinds, own)], soot_out.at[:, :, lanes], load_sem.at[1 + blocks + b]))
+        stores.append(pltpu.make_async_copy(result.at[b, pl.ds(0, kinds)], species_out.at[:, :, lanes], sem.at[b]))
+        stores.append(pltpu.make_async_copy(result.at[b, pl.ds(kinds, own)], soot_out.at[:, :, lanes], sem.at[blocks + b]))
     for copy in stores:
         copy.start()
-    for step in range(1, nsec):
-        p = (me + step) % nsec
-        sent(p, step).wait_send()
-        rate_copy(p, me, step).wait_send()
-        used_copy(p, me, step).wait_send()
     for copy in stores:
         copy.wait()
+
+
+def stay(x):
+    return pltpu.with_memory_space_constraint(x, pltpu.HBM)
 
 
 def shards(soot, species, kern, split, target, growth, diffusivity, reaction, stoich):
@@ -256,14 +310,14 @@
     count = -(-(kinds + own) // 8) * 8
     assert blocks * (rows // 8) == nsec and sections <= 128 and 3 * kinds <= 128
     dma = pltpu.SemaphoreType.DMA
-    hbm = pl.BlockSpec(memory_space=pl.ANY)
-    return pl.pallas_call(
+    hbm = pl.BlockSpec(memory_space=pltpu.HBM)
+    vmem = pl.BlockSpec(memory_space=pltpu.VMEM)
+    parts = pl.pallas_call(
         functools.partial(kernel, nsec, nxs, own, kinds),
-        out_shape=(jax.ShapeDtypeStruct(soot.shape, F32), jax.ShapeDtypeStruct(species.shape, F32)),
-        in_specs=[hbm] * 8 + [pl.BlockSpec(memory_space=pltpu.SMEM)],
-        out_specs=(hbm, hbm),
+        out_shape=jax.ShapeDtypeStruct((blocks, count, rows, 128), F32),
+        in_specs=[hbm] * 9,
+        out_specs=vmem,
         scratch_shapes=[
-            pltpu.VMEM((blocks, count, rows, 128), F32),
             pltpu.VMEM((blocks, count, rows, 128), F32),
             pltpu.VMEM((sections + 2 * PAD, 8, 128), F32),
             pltpu.VMEM((sections, 8, 128), F32),
@@ -278,16 +332,25 @@
             pltpu.VMEM(growth.shape, F32),
             pltpu.VMEM(diffusivity.shape, F32),
             pltpu.VMEM(reaction.shape, F32),
+            pltpu.SMEM(stoich.shape, F32),
             pltpu.VMEM((count, 128), F32),
             pltpu.VMEM((SLOTS, sections + 2 * PAD, 128), F32),
             pltpu.VMEM((SLOTS * sections, 384), BF16),
-            dma((1 + 2 * blocks + 6,)),
-            dma((nsec,)), dma((nsec,)), dma((nsec,)), dma((nsec,)), dma((nsec,)), dma((nsec,)),
-            dma((2,)), dma((2,)),
+            dma((1 + 2 * blocks + 7,)),
+            *[dma((PARTS, nsec))] * 6,
+            dma((2,)), dma((2,)), pltpu.SemaphoreType.REGULAR,
         ],
         compiler_params=pltpu.CompilerParams(
             collective_id=0, has_side_effects=True, vmem_limit_bytes=32 << 20),
-    )(soot, species, kern, split, target, growth, diffusivity, reaction, stoich)
+    )(*(stay(x) for x in (soot, species, kern, split, target, growth, diffusivity, reaction, stoich)))
+    return pl.pallas_call(
+        functools.partial(write_out, own, kinds),
+        out_shape=(jax.ShapeDtypeStruct(soot.shape, F32), jax.ShapeDtypeStruct(species.shape, F32)),
+        in_specs=[vmem],
+        out_specs=(hbm, hbm),
+        scratch_shapes=[dma((2 * blocks,))],
+        compiler_params=pltpu.CompilerParams(vmem_limit_bytes=4 << 20),
+    )(parts)
 
 
 def solution(mesh):

time: 49.2 us -> 33.2 us (0.67)
  the two profiles are of different devices: /device:TPU:16 before, /device:TPU:1 now
where the time goes in v3:
time: 33.2 us; the launch traced here: 32.8 us
  Pallas kernels  32.2 us (97%)
  between operations  0.64 us (2%)
    pallas_call x1, Pallas kernels, shards(): pl.pallas_call(functools.partial(kernel, nsec, nxs, own, kinds), out_shap...  30.4 us
    pallas_call x1, Pallas kernels, shards(): pl.pallas_call(functools.partial(write_out, own, kinds), out_shape=(jax.S...  1.73 us

profile of v3, /device:TPU:1, one launch (start us, length us, event | category | flops | bytes accessed | tf_op | source)
XLA Modules:
  0.0 32.8 jit_solution(9827866979459677466)
XLA Ops:
  0.6 30.4 %shard_map.104.result = f32[8,48,16,128]{3,2,1,0:T(8,128)S(1)} custom-call(f32[6,16,1024]{2,1,0:T(8,128)} %soot.1, f32[40,16,1024]{2,1,0:T(8,128)} %species.1, f32[96,96]{1,0:T(8,128)} %kern.1, f32[96,96]{1,0:T(8,128)} %split.1, s32[96,96]{1,0:T(8,128)} %target.1, f32[96]{0:T(128)} %growth.1, f32[40]{0:T(128)} %diffusivity.1, f32[40,40]{1,0:T(8,128)} %reaction.1, ...), custom_call_target="tpu_custom_call" | custom-call | tf_op jit(solution)/shard_map/pallas_call | solution.py:315
  31.1 1.7 %shard_map.105 = (f32[6,16,1024]{2,1,0:T(8,128)}, f32[40,16,1024]{2,1,0:T(8,128)}) custom-call(f32[8,48,16,128]{3,2,1,0:T(8,128)S(1)} %shard_map.104.result), custom_call_target="tpu_custom_call" | custom-call | tf_op jit(solution)/shard_map/pallas_call | solution.py:346

commit v4 on v3

--- a/solution.py
+++ b/solution.py
@@ -13,6 +13,7 @@
 PART = 4
 PARTS = 8 // PART
 ROWS_BEFORE = (5, 10)
+USED_ORDER = (4, 3, 5, 2, 6, 1, 7)
 ORDER = (3, 13, 11, 5, 4, 12, 2, 14, 10, 6, 1, 15, 9, 7, 8)
 LOW, HIGH = -1, 4
 SLOTS = HIGH - LOW + 1
@@ -79,16 +80,24 @@
         pl.semaphore_wait(barrier, nsec)
         pl.semaphore_signal(ready, inc=1, device_id={"xs": before}, device_id_type=MESH)
 
-    def cells(p, source, step, part):
+    def cells(p, source, part):
         return pltpu.make_async_remote_copy(
             src_ref=soot.at[:, part_rows(p, part), lanes_of(p)],
             dst_ref=dense.at[pl.ds(PAD + own * source, own), pl.ds(part * PART, PART)],
-            send_sem=send_sem.at[part, step], recv_sem=recv_sem.at[part, source],
+            send_sem=send_sem.at[part], recv_sem=recv_sem.at[part],
             device_id={"sec": p}, device_id_type=MESH)
+
+    peers = pl.ds(PAD, own * (nsec - 1))
+
+    def all_cells(part):
+        piece = dense.at[peers, pl.ds(part * PART, PART)]
+        return pltpu.make_async_remote_copy(
+            src_ref=piece, dst_ref=piece, send_sem=send_sem.at[part], recv_sem=recv_sem.at[part],
+            device_id={"sec": (me + 1) % nsec}, device_id_type=MESH)
 
     for part in range(PARTS):
         for step in ORDER:
-            cells((me + step) % nsec, me, step, part).start()
+            cells((me + step) % nsec, me, part).start()
 
     zero_tiles = jnp.zeros((PAD, 8, 128), F32)
     dense[0:PAD] = zero_tiles
@@ -210,41 +219,61 @@
             flat_rate[pl.ds(r, sections, stride=8), :] = total[:, n * 128:(n + 1) * 128]
             used[r:r + 1, :] = eaten[:, n * 128:(n + 1) * 128]
 
-    def rate_copy(p, source, step, part):
+    def rate_copy(p, source, part):
         return pltpu.make_async_remote_copy(
             src_ref=rate.at[pl.ds(own * p, own), pl.ds(part * PART, PART)],
             dst_ref=rate_in.at[source % blocks, :, part_rows(source, part), :],
-            send_sem=back_send.at[part, step], recv_sem=back_recv.at[part, source],
+            send_sem=back_send.at[part], recv_sem=back_recv.at[part],
             device_id={"sec": p}, device_id_type=MESH)
 
-    def used_copy(p, source, step, part):
-        return pltpu.make_async_remote_copy(
-            src_ref=used.at[pl.ds(part * PART, PART)],
-            dst_ref=used_in.at[source % blocks, part_rows(source, part), :],
-            send_sem=used_send.at[part, step], recv_sem=used_recv.at[part, source],
-            device_id={"sec": p}, device_id_type=MESH)
+    def all_rates(part):
+        piece = rate.at[pl.ds(0, own * (nsec - 1)), pl.ds(part * PART, PART)]
+        return pltpu.make_async_remote_copy(
+            src_ref=piece, dst_ref=piece, send_sem=back_send.at[part], recv_sem=back_recv.at[part],
+            device_id={"sec": (me + 1) % nsec}, device_id_type=MESH)
+
+    plane, place = me // blocks, me % blocks
+    planes = nsec // blocks
+
+    def used_copy(step):
+        return pltpu.make_async_remote_copy(
+            src_ref=used, dst_ref=used_in.at[place, tile_rows(me), :],
+            send_sem=used_send.at[0], recv_sem=used_recv.at[0],
+            device_id={"sec": plane * blocks + (place + step) % blocks}, device_id_type=MESH)
+
+    def all_used():
+        piece = used_in.at[pl.ds(0, blocks - 1), pl.ds(0, 8), :]
+        return pltpu.make_async_remote_copy(
+            src_ref=piece, dst_ref=piece, send_sem=used_send.at[0], recv_sem=used_recv.at[0],
+            device_id={"sec": plane * blocks + (place + 1) % blocks}, device_id_type=MESH)
+
+    def pass_on(step, source):
+        piece = used_in.at[:, pl.ds(pl.multiple_of(source * 8, 8), 8), :]
+        return pltpu.make_async_remote_copy(
+            src_ref=piece, dst_ref=piece,
+            send_sem=used_send.at[step], recv_sem=used_recv.at[step],
+            device_id={"sec": (plane + step) % planes * blocks + place}, device_id_type=MESH)
 
     first = 1
     for part in range(PARTS):
         last = ROWS_BEFORE[part]
         lax.fori_loop(first, last, inner, 0)
         first = last
-        for step in range(1, nsec):
-            p = (me + step) % nsec
-            cells(p, p, step, part).wait_recv()
+        all_cells(part).wait_recv()
         for pair in range(part * PART // 2, (part + 1) * PART // 2):
             rate_pair(pair)
+        if part == PARTS - 1:
+            used_in[place, tile_rows(me), :] = used[...]
+            for step in USED_ORDER:
+                used_copy(step).start()
         for step in ORDER:
-            used_copy((me + step) % nsec, me, step, part).start()
-        for step in ORDER:
-            rate_copy((me + step) % nsec, me, step, part).start()
+            rate_copy((me + step) % nsec, me, part).start()
         if part == 0:
             @pl.when(at < nxs - 1)
             def _():
                 pl.semaphore_wait(ready, 1)
                 edge(1).start()
     rate_in[me % blocks, :, tile_rows(me), :] = rate[pl.ds(own * me, own)]
-    used_in[me % blocks, tile_rows(me), :] = used[...]
 
     lax.fori_loop(first, rows - 1, inner, 0)
 
@@ -261,10 +290,11 @@
     row_step(0, edge_in[1], row_of(1))
     row_step(rows - 1, row_of(rows - 2), edge_in[0])
 
-    for part in range(PARTS):
-        for step in range(1, nsec):
-            p = (me + step) % nsec
-            used_copy(p, p, step, part).wait_recv()
+    all_used().wait_recv()
+    for step in range(1, planes):
+        pass_on(step, plane).start()
+    for step in range(1, planes):
+        pass_on(step, (plane - step + planes) % planes).wait_recv()
 
     def consume(s, carry):
         result[:, s] = result[:, s] - stoich_s[s] * used_in[...]
@@ -272,16 +302,14 @@
 
     lax.fori_loop(0, kinds, consume, 0)
     for part in range(PARTS):
-        for step in range(1, nsec):
-            p = (me + step) % nsec
-            rate_copy(p, p, step, part).wait_recv()
+        all_rates(part).wait_recv()
     result[:, kinds:kinds + own] = result[:, kinds:kinds + own] + rate_in[...]
     for part in range(PARTS):
-        for step in range(1, nsec):
-            p = (me + step) % nsec
-            cells(p, me, step, part).wait_send()
-            rate_copy(p, me, step, part).wait_send()
-            used_copy(p, me, step, part).wait_send()
+        all_cells(part).wait_send()
+        all_rates(part).wait_send()
+    all_used().wait_send()
+    for step in range(1, planes):
+        pass_on(step, plane).wait_send()
 
 
 def write_out(own, kinds, result, soot_out, species_out, sem):
@@ -337,7 +365,7 @@
             pltpu.VMEM((SLOTS, sections + 2 * PAD, 128), F32),
             pltpu.VMEM((SLOTS * sections, 384), BF16),
             dma((1 + 2 * blocks + 7,)),
-            *[dma((PARTS, nsec))] * 6,
+            *[dma((PARTS,))] * 4, *[dma((nsec // blocks,))] * 2,
             dma((2,)), dma((2,)), pltpu.SemaphoreType.REGULAR,
         ],
         compiler_params=pltpu.CompilerParams(

time: 33.2 us -> 32.2 us (0.970)
  the two profiles are of different devices: /device:TPU:1 before, /device:TPU:262 now
where the time goes in v4:
time: 32.2 us; the launch traced here: 32.1 us
  Pallas kernels  31.4 us (98%)
  between operations  0.64 us (2%)
    pallas_call x1, Pallas kernels, shards(): pl.pallas_call(functools.partial(kernel, nsec, nxs, own, kinds), out_shap...  29.7 us
    pallas_call x1, Pallas kernels, shards(): pl.pallas_call(functools.partial(write_out, own, kinds), out_shape=(jax.S...  1.73 us

profile of v4, /device:TPU:262, one launch (start us, length us, event | category | flops | bytes accessed | tf_op | source)
XLA Modules:
  0.0 32.1 jit_solution(13901424366055379067)
XLA Ops:
  0.6 29.7 %shard_map.104.result = f32[8,48,16,128]{3,2,1,0:T(8,128)S(1)} custom-call(f32[6,16,1024]{2,1,0:T(8,128)} %soot.1, f32[40,16,1024]{2,1,0:T(8,128)} %species.1, f32[96,96]{1,0:T(8,128)} %kern.1, f32[96,96]{1,0:T(8,128)} %split.1, s32[96,96]{1,0:T(8,128)} %target.1, f32[96]{0:T(128)} %growth.1, f32[40]{0:T(128)} %diffusivity.1, f32[40,40]{1,0:T(8,128)} %reaction.1, ...), custom_call_target="tpu_custom_call" | custom-call | tf_op jit(solution)/shard_map/pallas_call | solution.py:343
  30.3 1.7 %shard_map.105 = (f32[6,16,1024]{2,1,0:T(8,128)}, f32[40,16,1024]{2,1,0:T(8,128)}) custom-call(f32[8,48,16,128]{3,2,1,0:T(8,128)S(1)} %shard_map.104.result), custom_call_target="tpu_custom_call" | custom-call | tf_op jit(solution)/shard_map/pallas_call | solution.py:374

commit v5 on v4

--- a/solution.py
+++ b/solution.py
@@ -12,8 +12,8 @@
 PAD = 8
 PART = 4
 PARTS = 8 // PART
+CUTS = 4
 ROWS_BEFORE = (5, 10)
-USED_ORDER = (4, 3, 5, 2, 6, 1, 7)
 ORDER = (3, 13, 11, 5, 4, 12, 2, 14, 10, 6, 1, 15, 9, 7, 8)
 LOW, HIGH = -1, 4
 SLOTS = HIGH - LOW + 1
@@ -27,8 +27,8 @@
 def kernel(
     nsec, nxs, own, kinds,
     soot, species, kern, split, target, growth, diffusivity, reaction, stoich,
-    result,
-    fields, dense, rate, used, rate_in, used_in,
+    species_v, soot_v,
+    fields, result, dense, rate, used, rate_in, used_in,
     edge_out, edge_in, kern_v, split_v, target_v, growth_v, diff_v, react_v, stoich_s,
     react_pad, weights, lhs,
     load_sem, send_sem, recv_sem, back_send, back_recv, used_send, used_recv, edge_send, edge_recv, ready,
@@ -43,7 +43,7 @@
     before, after = (at + nxs - 1) % nxs, (at + 1) % nxs
 
     barrier = pltpu.get_barrier_semaphore()
-    for step in range(1, nsec):
+    for step in ORDER:
         pl.semaphore_signal(barrier, inc=1, device_id={"sec": (me + step) % nsec}, device_id_type=MESH)
 
     @pl.when(at < nxs - 1)
@@ -68,9 +68,6 @@
     tables = [(kern, kern_v), (split, split_v), (target, target_v), (growth, growth_v), (diffusivity, diff_v), (reaction, react_v), (stoich, stoich_s)]
     for n, (src, dst) in enumerate(tables):
         loads.append(pltpu.make_async_copy(src, dst, load_sem.at[1 + 2 * blocks + n]))
-    for copy in loads:
-        copy.start()
-
     @pl.when(at == 0)
     def _():
         pl.semaphore_wait(barrier, nsec - 1)
@@ -95,9 +92,13 @@
             src_ref=piece, dst_ref=piece, send_sem=send_sem.at[part], recv_sem=recv_sem.at[part],
             device_id={"sec": (me + 1) % nsec}, device_id_type=MESH)
 
-    for part in range(PARTS):
+    def send_cells(part):
         for step in ORDER:
             cells((me + step) % nsec, me, part).start()
+
+    send_cells(0)
+    for copy in loads:
+        copy.start()
 
     zero_tiles = jnp.zeros((PAD, 8, 128), F32)
     dense[0:PAD] = zero_tiles
@@ -160,6 +161,9 @@
     grow_col = jnp.sum(jnp.where(i == j, grow, 0.0), axis=1, keepdims=True)
     grow_prev = jnp.sum(jnp.where(i == j + 1, grow, 0.0), axis=1, keepdims=True)
 
+    for part in range(1, PARTS):
+        send_cells(part)
+
     fi = lax.broadcasted_iota(jnp.int32, (count, kinds), 0)
     fj = lax.broadcasted_iota(jnp.int32, (count, kinds), 1)
     diff_col = jnp.sum(jnp.where(fi == fj, diff_v[...].reshape(1, kinds), 0.0), axis=1, keepdims=True)
@@ -232,27 +236,17 @@
             src_ref=piece, dst_ref=piece, send_sem=back_send.at[part], recv_sem=back_recv.at[part],
             device_id={"sec": (me + 1) % nsec}, device_id_type=MESH)
 
-    plane, place = me // blocks, me % blocks
-    planes = nsec // blocks
-
-    def used_copy(step):
-        return pltpu.make_async_remote_copy(
-            src_ref=used, dst_ref=used_in.at[place, tile_rows(me), :],
-            send_sem=used_send.at[0], recv_sem=used_recv.at[0],
-            device_id={"sec": plane * blocks + (place + step) % blocks}, device_id_type=MESH)
-
-    def all_used():
-        piece = used_in.at[pl.ds(0, blocks - 1), pl.ds(0, 8), :]
-        return pltpu.make_async_remote_copy(
-            src_ref=piece, dst_ref=piece, send_sem=used_send.at[0], recv_sem=used_recv.at[0],
-            device_id={"sec": plane * blocks + (place + 1) % blocks}, device_id_type=MESH)
-
-    def pass_on(step, source):
-        piece = used_in.at[:, pl.ds(pl.multiple_of(source * 8, 8), 8), :]
-        return pltpu.make_async_remote_copy(
-            src_ref=piece, dst_ref=piece,
-            send_sem=used_send.at[step], recv_sem=used_recv.at[step],
-            device_id={"sec": (plane + step) % planes * blocks + place}, device_id_type=MESH)
+    def used_copy(p, part):
+        return pltpu.make_async_remote_copy(
+            src_ref=used.at[pl.ds(part * PART, PART)], dst_ref=used_in.at[me % blocks, part_rows(me, part), :],
+            send_sem=used_send.at[part], recv_sem=used_recv.at[part],
+            device_id={"sec": p}, device_id_type=MESH)
+
+    def all_used(part):
+        piece = dense.at[pl.ds(PAD, nsec - 1), pl.ds(part * PART, PART)]
+        return pltpu.make_async_remote_copy(
+            src_ref=piece, dst_ref=piece, send_sem=used_send.at[part], recv_sem=used_recv.at[part],
+            device_id={"sec": (me + 1) % nsec}, device_id_type=MESH)
 
     first = 1
     for part in range(PARTS):
@@ -262,10 +256,8 @@
         all_cells(part).wait_recv()
         for pair in range(part * PART // 2, (part + 1) * PART // 2):
             rate_pair(pair)
-        if part == PARTS - 1:
-            used_in[place, tile_rows(me), :] = used[...]
-            for step in USED_ORDER:
-                used_copy(step).start()
+        for step in ORDER:
+            used_copy((me + step) % nsec, part).start()
         for step in ORDER:
             rate_copy((me + step) % nsec, me, part).start()
         if part == 0:
@@ -273,6 +265,7 @@
             def _():
                 pl.semaphore_wait(ready, 1)
                 edge(1).start()
+    used_in[me % blocks, tile_rows(me), :] = used[...]
     rate_in[me % blocks, :, tile_rows(me), :] = rate[pl.ds(own * me, own)]
 
     lax.fori_loop(first, rows - 1, inner, 0)
@@ -290,35 +283,32 @@
     row_step(0, edge_in[1], row_of(1))
     row_step(rows - 1, row_of(rows - 2), edge_in[0])
 
-    all_used().wait_recv()
-    for step in range(1, planes):
-        pass_on(step, plane).start()
-    for step in range(1, planes):
-        pass_on(step, (plane - step + planes) % planes).wait_recv()
+    for part in range(PARTS):
+        all_used(part).wait_recv()
 
     def consume(s, carry):
-        result[:, s] = result[:, s] - stoich_s[s] * used_in[...]
+        for b in range(blocks):
+            species_v[s, :, b * 128:(b + 1) * 128] = result[b, s] - stoich_s[s] * used_in[b]
         return carry
 
     lax.fori_loop(0, kinds, consume, 0)
     for part in range(PARTS):
         all_rates(part).wait_recv()
-    result[:, kinds:kinds + own] = result[:, kinds:kinds + own] + rate_in[...]
+    for b in range(blocks):
+        soot_v[:, :, b * 128:(b + 1) * 128] = result[b, kinds:kinds + own] + rate_in[b]
     for part in range(PARTS):
         all_cells(part).wait_send()
         all_rates(part).wait_send()
-    all_used().wait_send()
-    for step in range(1, planes):
-        pass_on(step, plane).wait_send()
-
-
-def write_out(own, kinds, result, soot_out, species_out, sem):
-    blocks = result.shape[0]
-    stores = []
-    for b in range(blocks):
-        lanes = pl.ds(b * 128, 128)
-        stores.append(pltpu.make_async_copy(result.at[b, pl.ds(0, kinds)], species_out.at[:, :, lanes], sem.at[b]))
-        stores.append(pltpu.make_async_copy(result.at[b, pl.ds(kinds, own)], soot_out.at[:, :, lanes], sem.at[blocks + b]))
+    for part in range(PARTS):
+        all_used(part).wait_send()
+
+
+def write_out(species_v, soot_v, species_out, soot_out, sem):
+    some = species_v.shape[0] // CUTS
+    stores = [
+        pltpu.make_async_copy(species_v.at[pl.ds(n * some, some)], species_out.at[pl.ds(n * some, some)], sem.at[n])
+        for n in range(CUTS)]
+    stores.append(pltpu.make_async_copy(soot_v, soot_out, sem.at[CUTS]))
     for copy in stores:
         copy.start()
     for copy in stores:
@@ -340,12 +330,14 @@
     dma = pltpu.SemaphoreType.DMA
     hbm = pl.BlockSpec(memory_space=pltpu.HBM)
     vmem = pl.BlockSpec(memory_space=pltpu.VMEM)
+    outs = (jax.ShapeDtypeStruct(species.shape, F32), jax.ShapeDtypeStruct(soot.shape, F32))
     parts = pl.pallas_call(
         functools.partial(kernel, nsec, nxs, own, kinds),
-        out_shape=jax.ShapeDtypeStruct((blocks, count, rows, 128), F32),
+        out_shape=outs,
         in_specs=[hbm] * 9,
-        out_specs=vmem,
+        out_specs=(vmem, vmem),
         scratch_shapes=[
+            pltpu.VMEM((blocks, count, rows, 128), F32),
             pltpu.VMEM((blocks, count, rows, 128), F32),
             pltpu.VMEM((sections + 2 * PAD, 8, 128), F32),
             pltpu.VMEM((sections, 8, 128), F32),
@@ -365,20 +357,21 @@
             pltpu.VMEM((SLOTS, sections + 2 * PAD, 128), F32),
             pltpu.VMEM((SLOTS * sections, 384), BF16),
             dma((1 + 2 * blocks + 7,)),
-            *[dma((PARTS,))] * 4, *[dma((nsec // blocks,))] * 2,
+            *[dma((PARTS,))] * 6,
             dma((2,)), dma((2,)), pltpu.SemaphoreType.REGULAR,
         ],
         compiler_params=pltpu.CompilerParams(
             collective_id=0, has_side_effects=True, vmem_limit_bytes=32 << 20),
     )(*(stay(x) for x in (soot, species, kern, split, target, growth, diffusivity, reaction, stoich)))
-    return pl.pallas_call(
-        functools.partial(write_out, own, kinds),
-        out_shape=(jax.ShapeDtypeStruct(soot.shape, F32), jax.ShapeDtypeStruct(species.shape, F32)),
-        in_specs=[vmem],
+    species_out, soot_out = pl.pallas_call(
+        write_out,
+        out_shape=outs,
+        in_specs=[vmem, vmem],
         out_specs=(hbm, hbm),
-        scratch_shapes=[dma((2 * blocks,))],
+        scratch_shapes=[dma((CUTS + 1,))],
         compiler_params=pltpu.CompilerParams(vmem_limit_bytes=4 << 20),
-    )(parts)
+    )(*parts)
+    return soot_out, species_out
 
 
 def solution(mesh):

time: 32.2 us -> 30.9 us (0.960)
  the two profiles are of different devices: /device:TPU:262 before, /device:TPU:1 now
where the time goes in v5:
time: 30.9 us; the launch traced here: 30.8 us
  Pallas kernels  30.1 us (97%)
  between operations  0.64 us (2%)
    pallas_call x1, Pallas kernels, shards(): pl.pallas_call(functools.partial(kernel, nsec, nxs, own, kinds), out_shap...  28.5 us
    pallas_call x1, Pallas kernels, shards(): pl.pallas_call(write_out, out_shape=outs, in_specs=[vmem, vmem], out_spec...  1.65 us

profile of v5, /device:TPU:1, one launch (start us, length us, event | category | flops | bytes accessed | tf_op | source)
XLA Modules:
  0.0 30.8 jit_solution(16921637700139215904)
XLA Ops:
  0.6 28.5 %shard_map.104 = (f32[40,16,1024]{2,1,0:T(8,128)S(1)}, f32[6,16,1024]{2,1,0:T(8,128)S(1)}) custom-call(f32[6,16,1024]{2,1,0:T(8,128)} %soot.1, f32[40,16,1024]{2,1,0:T(8,128)} %species.1, f32[96,96]{1,0:T(8,128)} %kern.1, f32[96,96]{1,0:T(8,128)} %split.1, s32[96,96]{1,0:T(8,128)} %target.1, f32[96]{0:T(128)} %growth.1, f32[40]{0:T(128)} %diffusivity.1, ...), custom_call_target="tpu_custom_call" | custom-call | tf_op jit(solution)/shard_map/pallas_call | solution.py:334
  29.1 1.7 %shard_map.105 = (f32[40,16,1024]{2,1,0:T(8,128)}, f32[6,16,1024]{2,1,0:T(8,128)}) custom-call(f32[40,16,1024]{2,1,0:T(8,128)S(1)} %get-tuple-element.6.species_v, f32[6,16,1024]{2,1,0:T(8,128)S(1)} %get-tuple-element.7.soot_v), custom_call_target="tpu_custom_call" | custom-call | tf_op jit(solution)/shard_map/pallas_call | solution.py:366

commit v6 on v5

--- a/solution.py
+++ b/solution.py
@@ -12,7 +12,7 @@
 PAD = 8
 PART = 4
 PARTS = 8 // PART
-CUTS = 4
+CUTS = 1
 ROWS_BEFORE = (5, 10)
 ORDER = (3, 13, 11, 5, 4, 12, 2, 14, 10, 6, 1, 15, 9, 7, 8)
 LOW, HIGH = -1, 4
@@ -256,10 +256,14 @@
         all_cells(part).wait_recv()
         for pair in range(part * PART // 2, (part + 1) * PART // 2):
             rate_pair(pair)
-        for step in ORDER:
-            used_copy((me + step) % nsec, part).start()
+        if part == PARTS - 1:
+            for step in ORDER:
+                used_copy((me + step) % nsec, part).start()
         for step in ORDER:
             rate_copy((me + step) % nsec, me, part).start()
+        if part < PARTS - 1:
+            for step in ORDER:
+                used_copy((me + step) % nsec, part).start()
         if part == 0:
             @pl.when(at < nxs - 1)
             def _():

time: 30.9 us -> 30.9 us (level)
  no operation moved by 1% of the time
where the time goes in v6:
time: 30.9 us; the launch traced here: 30.8 us
  Pallas kernels  30.1 us (97%)
  between operations  0.64 us (2%)
    pallas_call x1, Pallas kernels, shards(): pl.pallas_call(functools.partial(kernel, nsec, nxs, own, kinds), out_shap...  28.5 us
    pallas_call x1, Pallas kernels, shards(): pl.pallas_call(write_out, out_shape=outs, in_specs=[vmem, vmem], out_spec...  1.63 us

profile of v6, /device:TPU:1, one launch (start us, length us, event | category | flops | bytes accessed | tf_op | source)
XLA Modules:
  0.0 30.8 jit_solution(2883717174039639053)
XLA Ops:
  0.6 28.5 %shard_map.104 = (f32[40,16,1024]{2,1,0:T(8,128)S(1)}, f32[6,16,1024]{2,1,0:T(8,128)S(1)}) custom-call(f32[6,16,1024]{2,1,0:T(8,128)} %soot.1, f32[40,16,1024]{2,1,0:T(8,128)} %species.1, f32[96,96]{1,0:T(8,128)} %kern.1, f32[96,96]{1,0:T(8,128)} %split.1, s32[96,96]{1,0:T(8,128)} %target.1, f32[96]{0:T(128)} %growth.1, f32[40]{0:T(128)} %diffusivity.1, ...), custom_call_target="tpu_custom_call" | custom-call | tf_op jit(solution)/shard_map/pallas_call | solution.py:338
  29.2 1.6 %shard_map.105 = (f32[40,16,1024]{2,1,0:T(8,128)}, f32[6,16,1024]{2,1,0:T(8,128)}) custom-call(f32[40,16,1024]{2,1,0:T(8,128)S(1)} %get-tuple-element.6.species_v, f32[6,16,1024]{2,1,0:T(8,128)S(1)} %get-tuple-element.7.soot_v), custom_call_target="tpu_custom_call" | custom-call | tf_op jit(solution)/shard_map/pallas_call | solution.py:370
